TPU v7x, 32 devices: a whole 2x2x4 slice. The times are simulated.
32 devices in a mesh: dp: 8 (over y, x, core), mp: 4 (over z).
Axes of the slice: x: 2, y: 2, z: 4, core: 2. Of those that a mesh axis runs over, the one named last changes fastest.
Arguments:
- tokens: bfloat16 [16, 512, 1024], P('dp', 'mp'), may hold values from -6 to 6
- memory: bfloat16 [16, 512, 1024], P('dp', 'mp'), may hold values from -6 to 6
- compressed: bfloat16 [16, 512, 1024], P('dp', 'mp'), may hold values from -6 to 6
- valid_counts: int32 [16], P('dp'), may hold values from 64 to 512, as said below
- attention_norm_gain: float32 [1024], replicated, may hold values from 0.5 to 1.5
- attention_norm_bias: float32 [1024], replicated, may hold values from -1.75 to 1.75
- query_projection: bfloat16 [1024, 1024], P(None, 'mp'), may hold values from -0.1875 to 0.1875
- key_projection: bfloat16 [1024, 1024], P(None, 'mp'), may hold values from -0.1875 to 0.1875
- value_projection: bfloat16 [1024, 1024], P(None, 'mp'), may hold values from -0.1875 to 0.1875
- out_weight: bfloat16 [1024, 1024], P('mp'), may hold values from -2 to 2
- feedforward_norm_gain: float32 [1024], replicated, may hold values from 0.5 to 1.5
- feedforward_norm_bias: float32 [1024], replicated, may hold values from -1.75 to 1.75
- up_weight: bfloat16 [1024, 4096], P(None, 'mp'), may hold values from -0.1875 to 0.1875
- up_bias: float32 [4096], P('mp'), may hold values from -3 to 3
- down_weight: bfloat16 [4096, 1024], P('mp'), may hold values from -0.09375 to 0.09375
- down_bias: float32 [1024], replicated, may hold values from -3 to 3
- squeeze_weight: bfloat16 [3072, 1024], replicated, may hold values from -0.109375 to 0.109375
- cotangent: bfloat16 [16, 512, 1024], P('dp', 'mp'), may hold values from -6 to 6
Outputs:
- output: bfloat16 [16, 512, 1024], P('dp', 'mp')
- tokens_grad: float32 [16, 512, 1024], P('dp', 'mp')
- attention_gain_gradient: float32 [1024], replicated
- first_bias_grad: float32 [1024], replicated
- query_weight_grad: float32 [1024, 1024], P(None, 'mp')
- key_weight_grad: float32 [1024, 1024], P(None, 'mp')
- value_weight_grad: float32 [1024, 1024], P(None, 'mp')
- out_weight_grad: float32 [1024, 1024], P('mp')
- feedforward_gain_gradient: float32 [1024], replicated
- second_bias_grad: float32 [1024], replicated
- up_weight_grad: float32 [1024, 4096], P(None, 'mp')
- up_bias_grad: float32 [4096], P('mp')
- down_weight_grad: float32 [4096, 1024], P('mp')
- down_bias_grad: float32 [1024], replicated
- new_memory: bfloat16 [16, 512, 1024], P('dp', 'mp')
- new_compressed: bfloat16 [16, 512, 1024], P('dp', 'mp')
Inputs may be any that keep to these rules, and one draw needn't show every extreme that they name: The first valid_counts tokens of a segment are real, the rest padding.
All inputs are finite; a program needn't handle non-finite values.
Results may differ from a plain program's by a relative error of at most 0.015.
Values may be sent and summed in bfloat16 or wider, within the bound.
A program may use at most 192 MiB of HBM per device.

v0:
```python
import jax
import jax.numpy as jnp
from jax import lax
from jax.sharding import PartitionSpec as P

HEAD_DIM = 128
RATE = 3


def apply_layer_norm(rows):
    center = jnp.mean(rows, axis=-1, keepdims=True)
    centered = rows - center
    spread = jnp.mean(centered * centered, axis=-1, keepdims=True)
    inverse_deviation = lax.rsqrt(spread + 1e-05)
    return (centered * inverse_deviation, inverse_deviation)


def norm_backward_pass(input_gradient, standardized_rows, inverse_deviation, scale_factor):
    scaled_rows = input_gradient * scale_factor
    attention_norm_mean = jnp.mean(scaled_rows, axis=-1, keepdims=True)
    feedforward_norm_mean = jnp.mean(scaled_rows * standardized_rows, axis=-1, keepdims=True)
    return inverse_deviation * (
        scaled_rows - attention_norm_mean - standardized_rows * feedforward_norm_mean
    )


def squeeze_rows(old_comp, old_mem, fresh, valid_count, offset, own_rows, squeeze_weight):
    features = old_mem.shape[1]
    joined = jnp.concatenate([old_mem, fresh], axis=0)
    new_memory = lax.dynamic_slice_in_dim(joined, valid_count + offset, own_rows, 0)
    comp_len = old_comp.shape[0]
    evicted = valid_count // RATE
    first_row = evicted + offset
    window_start = jnp.maximum(first_row - comp_len, 0)
    padded = jnp.concatenate(
        [old_mem, jnp.zeros((RATE * own_rows, features), jnp.bfloat16)], axis=0
    )
    window = lax.dynamic_slice_in_dim(padded, window_start * RATE, RATE * own_rows, 0)
    squeezed = jnp.dot(
        window.reshape(own_rows, RATE * features),
        squeeze_weight,
        preferred_element_type=jnp.float32,
    ).astype(jnp.bfloat16)
    positions = first_row + jnp.arange(own_rows)
    from_old = jnp.take(old_comp, jnp.clip(positions, 0, comp_len - 1), axis=0)
    from_new = jnp.take(
        squeezed, jnp.clip(positions - comp_len - window_start, 0, own_rows - 1), axis=0
    )
    new_compressed = jnp.where((positions < comp_len)[:, None], from_old, from_new)
    return (new_memory, new_compressed)


def per_device(
    tokens,
    memory,
    compressed,
    valid_counts,
    attention_norm_gain,
    attention_norm_bias,
    query_projection,
    key_projection,
    value_projection,
    out_weight,
    feedforward_norm_gain,
    feedforward_norm_bias,
    up_weight,
    up_bias,
    down_weight,
    down_bias,
    squeeze_weight,
    cotangent,
):
    batch_segs, own_rows, features = tokens.shape
    offset = lax.axis_index("mp") * own_rows
    old_comp, old_mem, fresh = (
        lax.all_gather(compressed, "mp", axis=1, tiled=True),
        lax.all_gather(memory, "mp", axis=1, tiled=True),
        lax.all_gather(tokens, "mp", axis=1, tiled=True),
    )
    seg_len = fresh.shape[1]
    prior_rows = old_comp.shape[1] + old_mem.shape[1]
    context_tokens = jnp.concatenate([old_comp, old_mem, fresh], axis=1).astype(jnp.float32)
    ctx_len = context_tokens.shape[1]
    standardized_full, inverse_deviation_full = apply_layer_norm(context_tokens)
    normed_rows = (standardized_full * attention_norm_gain + attention_norm_bias).astype(
        jnp.bfloat16
    )
    token_rows_normed = normed_rows[:, prior_rows:]
    queries = jnp.einsum(
        "xhp,pj->xhj", token_rows_normed, query_projection, preferred_element_type=jnp.float32
    ).astype(jnp.bfloat16)
    key_rows = jnp.einsum(
        "xhp,pj->xhj", normed_rows, key_projection, preferred_element_type=jnp.float32
    ).astype(jnp.bfloat16)
    values = jnp.einsum(
        "xhp,pj->xhj", normed_rows, value_projection, preferred_element_type=jnp.float32
    ).astype(jnp.bfloat16)
    local_heads = query_projection.shape[1] // HEAD_DIM
    score_scale = HEAD_DIM ** (-0.5)

    def by_heads(matrix):
        return matrix.reshape(matrix.shape[0], matrix.shape[1], local_heads, HEAD_DIM)

    query_pos = jnp.arange(seg_len)[:, None]
    key_pos = jnp.arange(ctx_len)[None, :] - prior_rows
    allowed = (key_pos[None] < 0) | (key_pos <= query_pos)[None] & (
        key_pos[None] < valid_counts[:, None, None]
    )

    def scores_of(query_in, key_in):
        raw = (
            jnp.einsum(
                "gqhe,gkhe->ghqk",
                by_heads(query_in),
                by_heads(key_in),
                preferred_element_type=jnp.float32,
            )
            * score_scale
        )
        return jnp.where(allowed[:, None], raw, -1e30)

    scores = scores_of(queries, key_rows)
    peak_score = jnp.max(scores, axis=-1, keepdims=True)
    exponent = jnp.exp(scores - peak_score)
    exp_total = jnp.sum(exponent, axis=-1, keepdims=True)
    log_total = peak_score + jnp.log(exp_total)
    probs_low = (exponent / exp_total).astype(jnp.bfloat16)
    mixed_heads = jnp.einsum(
        "ghqk,gkhe->gqhe", probs_low, by_heads(values), preferred_element_type=jnp.float32
    ).astype(jnp.bfloat16)
    mixed_heads = mixed_heads.reshape(batch_segs, seg_len, local_heads * HEAD_DIM)
    partial_attn = jnp.einsum(
        "gsc,cd->gsd", mixed_heads, out_weight, preferred_element_type=jnp.float32
    )
    attention = lax.psum_scatter(partial_attn, "mp", scatter_dimension=1, tiled=True)
    residual_stream = tokens.astype(jnp.float32) + attention
    standardized_feedforward, inverse_deviation_feedforward = apply_layer_norm(residual_stream)
    feedforward_input = (
        standardized_feedforward * feedforward_norm_gain + feedforward_norm_bias
    ).astype(jnp.bfloat16)
    second_all = lax.all_gather(feedforward_input, "mp", axis=1, tiled=True)
    upper_in = (
        jnp.einsum("gsd,df->gsf", second_all, up_weight, preferred_element_type=jnp.float32)
        + up_bias
    )
    active, gelu_back = jax.vjp(jax.nn.gelu, upper_in)
    active_low = active.astype(jnp.bfloat16)
    partial_ffn = jnp.einsum(
        "gsf,fd->gsd", active_low, down_weight, preferred_element_type=jnp.float32
    )
    down_out = lax.psum_scatter(
        partial_ffn.astype(jnp.bfloat16), "mp", scatter_dimension=1, tiled=True
    ).astype(jnp.float32)
    output = (residual_stream + down_out + down_bias).astype(jnp.bfloat16)

    def update_one(comp_seg, mem_seg, fresh_seg, valid_count):
        return squeeze_rows(
            comp_seg, mem_seg, fresh_seg, valid_count, offset, own_rows, squeeze_weight
        )

    new_memory, new_compressed = jax.vmap(update_one)(old_comp, old_mem, fresh, valid_counts)
    output_gradient = cotangent.astype(jnp.float32)
    down_bias_grad = jnp.sum(output_gradient, axis=(0, 1))
    grad_all = lax.all_gather(cotangent, "mp", axis=1, tiled=True)
    down_weight_grad = jnp.einsum(
        "gsf,gsd->fd", active_low, grad_all, preferred_element_type=jnp.float32
    )
    grad_active = jnp.einsum(
        "gsd,fd->gsf", grad_all, down_weight, preferred_element_type=jnp.float32
    )
    grad_upper = gelu_back(grad_active)[0].astype(jnp.bfloat16)
    up_weight_grad = jnp.einsum(
        "gsd,gsf->df", second_all, grad_upper, preferred_element_type=jnp.float32
    )
    up_bias_grad = jnp.sum(grad_upper.astype(jnp.float32), axis=(0, 1))
    partial_second = jnp.einsum(
        "gsf,df->gsd", grad_upper, up_weight, preferred_element_type=jnp.float32
    )
    feedforward_gradient = lax.psum_scatter(partial_second, "mp", scatter_dimension=1, tiled=True)
    feedforward_gain_gradient = jnp.sum(
        feedforward_gradient * standardized_feedforward, axis=(0, 1)
    )
    second_bias_grad = jnp.sum(feedforward_gradient, axis=(0, 1))
    residual_gradient = output_gradient + norm_backward_pass(
        feedforward_gradient,
        standardized_feedforward,
        inverse_deviation_feedforward,
        feedforward_norm_gain,
    )
    grad_resid_all = lax.all_gather(
        residual_gradient.astype(jnp.bfloat16), "mp", axis=1, tiled=True
    )
    out_weight_grad = jnp.einsum(
        "gsc,gsd->cd", mixed_heads, grad_resid_all, preferred_element_type=jnp.float32
    )
    grad_mixed = jnp.einsum(
        "gsd,cd->gsc", grad_resid_all, out_weight, preferred_element_type=jnp.float32
    ).astype(jnp.bfloat16)
    probs_again = jnp.exp(scores_of(queries, key_rows) - log_total)
    grad_probs = jnp.einsum(
        "gqhe,gkhe->ghqk",
        by_heads(grad_mixed),
        by_heads(values),
        preferred_element_type=jnp.float32,
    )
    row_dot = jnp.sum(probs_again * grad_probs, axis=-1, keepdims=True)
    grad_scores = (probs_again * (grad_probs - row_dot)).astype(jnp.bfloat16)
    query_gradient = (
        score_scale
        * jnp.einsum(
            "ghqk,gkhe->gqhe", grad_scores, by_heads(key_rows), preferred_element_type=jnp.float32
        )
    ).astype(jnp.bfloat16)
    key_gradient = (
        score_scale
        * jnp.einsum(
            "ghqk,gqhe->gkhe", grad_scores, by_heads(queries), preferred_element_type=jnp.float32
        )
    ).astype(jnp.bfloat16)
    value_gradient = jnp.einsum(
        "ghqk,gqhe->gkhe",
        probs_again.astype(jnp.bfloat16),
        by_heads(grad_mixed),
        preferred_element_type=jnp.float32,
    ).astype(jnp.bfloat16)
    query_gradient = query_gradient.reshape(batch_segs, seg_len, -1)
    key_gradient = key_gradient.reshape(batch_segs, ctx_len, -1)
    value_gradient = value_gradient.reshape(batch_segs, ctx_len, -1)
    query_weight_grad = jnp.einsum(
        "nja,njr->ar", token_rows_normed, query_gradient, preferred_element_type=jnp.float32
    )
    key_weight_grad = jnp.einsum(
        "nja,njr->ar", normed_rows, key_gradient, preferred_element_type=jnp.float32
    )
    value_weight_grad = jnp.einsum(
        "nja,njr->ar", normed_rows, value_gradient, preferred_element_type=jnp.float32
    )
    partial_normed = jnp.einsum(
        "xmo,qo->xmq", key_gradient, key_projection, preferred_element_type=jnp.float32
    )
    partial_normed = partial_normed + jnp.einsum(
        "xmo,qo->xmq", value_gradient, value_projection, preferred_element_type=jnp.float32
    )
    partial_normed = partial_normed.at[:, prior_rows:].add(
        jnp.einsum(
            "xmo,qo->xmq", query_gradient, query_projection, preferred_element_type=jnp.float32
        )
    )
    partial_normed = partial_normed.reshape(batch_segs, 3, seg_len, features)
    normed_gradient = lax.psum_scatter(
        partial_normed.astype(jnp.bfloat16), "mp", scatter_dimension=2, tiled=True
    ).astype(jnp.float32)
    segment_context = jnp.stack([compressed, memory, tokens], axis=1).astype(jnp.float32)
    standardized_segment, inverse_deviation_segment = apply_layer_norm(segment_context)
    attention_gain_gradient = jnp.sum(normed_gradient * standardized_segment, axis=(0, 1, 2))
    first_bias_grad = jnp.sum(normed_gradient, axis=(0, 1, 2))
    tokens_grad = residual_gradient + norm_backward_pass(
        normed_gradient[:, 2],
        standardized_segment[:, 2],
        inverse_deviation_segment[:, 2],
        attention_norm_gain,
    )
    summed = (
        lax.psum(query_weight_grad.astype(jnp.bfloat16), "dp").astype(jnp.float32),
        lax.psum(key_weight_grad.astype(jnp.bfloat16), "dp").astype(jnp.float32),
        lax.psum(value_weight_grad.astype(jnp.bfloat16), "dp").astype(jnp.float32),
        lax.psum(out_weight_grad.astype(jnp.bfloat16), "dp").astype(jnp.float32),
        lax.psum(up_weight_grad.astype(jnp.bfloat16), "dp").astype(jnp.float32),
        lax.psum(up_bias_grad.astype(jnp.bfloat16), "dp").astype(jnp.float32),
        lax.psum(down_weight_grad.astype(jnp.bfloat16), "dp").astype(jnp.float32),
    )
    norms = lax.psum(
        (
            attention_gain_gradient,
            first_bias_grad,
            feedforward_gain_gradient,
            second_bias_grad,
            down_bias_grad,
        ),
        ("dp", "mp"),
    )
    return (
        output,
        tokens_grad,
        norms[0],
        norms[1],
        summed[0],
        summed[1],
        summed[2],
        summed[3],
        norms[2],
        norms[3],
        summed[4],
        summed[5],
        summed[6],
        norms[4],
        new_memory,
        new_compressed,
    )


def solution(mesh):
    in_specs = (
        P("dp", "mp", None),
        P("dp", "mp", None),
        P("dp", "mp", None),
        P("dp"),
        P(),
        P(),
        P(None, "mp"),
        P(None, "mp"),
        P(None, "mp"),
        P("mp", None),
        P(),
        P(),
        P(None, "mp"),
        P("mp"),
        P("mp", None),
        P(),
        P(),
        P("dp", "mp", None),
    )
    out_specs = (
        P("dp", "mp", None),
        P("dp", "mp", None),
        P(),
        P(),
        P(None, "mp"),
        P(None, "mp"),
        P(None, "mp"),
        P("mp", None),
        P(),
        P(),
        P(None, "mp"),
        P("mp"),
        P("mp", None),
        P(),
        P("dp", "mp", None),
        P("dp", "mp", None),
    )
    return jax.shard_map(
        per_device, mesh=mesh, in_specs=in_specs, out_specs=out_specs, check_vma=False
    )
```

profile of v0, /device:TPU:0, one launch (start us, length us, event | category | flops | bytes accessed | tf_op | source)
XLA Modules:
  0.0 852.4 jit_solution(12164202690082199267)
XLA Ops:
  12.8 45.5 %all-gather.9.cloned.1.call-done = bf16[2,512,1024]{2,1,0:T(8,128)(2,1)} async-done(((bf16[2,128,1024]{2,1,0:T(8,128)(2,1)}), bf16[2,512,1024]{2,1,0:T(8,128)(2,1)}) %all-gather.9.cloned.1.call-update) | async-done | bytes 2097168 | tf_op jit(solution)/shard_map/all_gather | solution.py:77
  58.3 46.3 %all-gather.7.cloned.1.call-done = bf16[2,512,1024]{2,1,0:T(8,128)(2,1)} async-done(((bf16[2,128,1024]{2,1,0:T(8,128)(2,1)}), bf16[2,512,1024]{2,1,0:T(8,128)(2,1)}) %all-gather.7.cloned.1.call-update) | async-done | bytes 2097168 | tf_op jit(solution)/shard_map/all_gather | solution.py:76
  104.5 46.3 %all-gather.11.cloned.1.call-done = bf16[2,512,1024]{2,1,0:T(8,128)(2,1)} async-done(((bf16[2,128,1024]{2,1,0:T(8,128)(2,1)}), bf16[2,512,1024]{2,1,0:T(8,128)(2,1)}) %all-gather.11.cloned.1.call-update) | async-done | bytes 2097168 | tf_op jit(solution)/shard_map/all_gather | solution.py:78
  150.8 4.9 convert_reduce_fusion
  155.8 5.4 fusion.2
  161.2 5.2 fusion.5
  169.2 3.1 convolution_convert_fusion.1
  172.4 3.2 fusion.90
  180.1 4.5 fusion.59
  185.4 2.7 fusion.63
  188.2 75.6 %reduce-scatter.5.cloned.1.call-done = f32[2,128,1024]{2,1,0:T(8,128)} async-done(((f32[2,512,1024]{2,1,0:T(8,128)}), f32[2,128,1024]{2,1,0:T(8,128)}) %reduce-scatter.5.cloned.1.call-update) | async-done | bytes 1048592 | tf_op jit(solution)/shard_map/reduce_scatter | solution.py:135
  267.3 46.0 %all-gather.13.cloned.1.call-done = bf16[2,512,1024]{2,1,0:T(8,128)(2,1)} async-done(((bf16[2,128,1024]{2,1,0:T(8,128)(2,1)}), bf16[2,512,1024]{2,1,0:T(8,128)(2,1)}) %all-gather.13.cloned.1.call-update) | async-done | bytes 2097168 | tf_op jit(solution)/shard_map/all_gather | solution.py:141
  313.3 6.6 fusion.34
  319.9 39.6 %all-gather.15.cloned.1.call-done = bf16[2,512,1024]{2,1,0:T(8,128)(2,1)} async-done(((bf16[2,128,1024]{2,1,0:T(8,128)(2,1)}), bf16[2,512,1024]{2,1,0:T(8,128)(2,1)}) %all-gather.15.cloned.1.call-update) | async-done | bytes 2097168 | tf_op jit(solution)/shard_map/all_gather | solution.py:164
  359.5 7.5 fusion.91
  368.3 4.4 fusion.32
  372.8 75.6 %reduce-scatter.9.cloned.1.call-done = f32[2,128,1024]{2,1,0:T(8,128)} async-done(((f32[2,512,1024]{2,1,0:T(8,128)}), f32[2,128,1024]{2,1,0:T(8,128)}) %reduce-scatter.9.cloned.1.call-update) | async-done | bytes 1048592 | tf_op jit(solution)/shard_map/reduce_scatter | solution.py:179
  453.1 6.1 bitcast_convert_fusion.1
  459.2 4.4 bitcast_convert_fusion
  463.6 35.6 %all-gather.17.cloned.1.call-done = bf16[2,512,1024]{2,1,0:T(8,128)(2,1)} async-done(((bf16[2,128,1024]{2,1,0:T(8,128)(2,1)}), bf16[2,512,1024]{2,1,0:T(8,128)(2,1)}) %all-gather.17.cloned.1.call-update) | async-done | bytes 2097168 | tf_op jit(solution)/shard_map/all_gather | solution.py:190
  501.7 7.0 fusion.26
  508.7 9.5 %multiply_reduce_fusion = (f32[2,2,512]{2,1,0:T(2,128)S(1)}, f32[2,2,512,1536]{3,2,1,0:T(8,128)}) fusion(f32[2,2,512,1536]{3,2,1,0:T(8,128)} %copy-done.1, f32[2,2,512]{2,1,0:T(2,128)S(1)} %log_add_fusion, bf16[2,512,2,128]{1,3,2,0:T(8,128)(2,1)S(1)} %bitcast.182, bf16[2,1536,2,128]{1,3,2,0:T(8,128)(2,1)S(1)} %bitcast.184), kind=kOutput, calls=%fused_computation.15 | convolution fusion | flops 814741504 | bytes 27279360 | tf_op jit(solution)/shard_map/gqhe,gkhe->ghqk/dot_general | solution.py:200
  518.2 6.4 multiply_convert_fusion
  532.9 2.7 fusion.47
  537.4 3.5 fusion.65
  540.9 6.4 convolution_add_fusion
  547.3 5.0 fusion.21
  552.3 8.4 convert_element_type.161
  560.8 6.8 copy.66
  571.7 6.4 fusion.36
  578.5 3.9 concatenate.20
  582.4 8.2 while.4
  583.0 3.5 dynamic-slice_dynamic-update-slice_fusion.5
  587.1 3.5 dynamic-slice_dynamic-update-slice_fusion.5
  590.6 3.7 reshape.419
  594.3 6.3 fusion.49
  600.7 8.1 gather_fusion.1
  608.7 4.1 gather_fusion
  612.9 5.3 pad_maximum_fusion.1
  619.2 7.3 while.3
  619.8 3.0 dynamic-slice_dynamic-update-slice_fusion.4
  623.4 3.0 dynamic-slice_dynamic-update-slice_fusion.4
  626.4 14.4 %psum.93 = bf16[1024]{0:T(1024)(128)(2,1)S(1)} all-reduce(bf16[1024]{0:T(1024)(128)(2,1)S(1)} %get-tuple-element.121), channel_id=1, replica_groups=mesh['dp'=8,'mp'=4] {'dp'}, use_global_device_ids=true, to_apply=%region_31.32 | all-reduce | flops 1024 | bytes 4096 | tf_op jit(solution)/shard_map/psum | solution.py:269
  649.0 2.6 convert_element_type.173
  654.1 100.5 %reduce-scatter.11.cloned.1.call-done = bf16[2,3,128,1024]{3,2,0,1:T(8,128)(2,1)} async-done(((bf16[2,3,512,1024]{3,2,0,1:T(8,128)(2,1)}), bf16[2,3,128,1024]{3,2,0,1:T(8,128)(2,1)}) %reduce-scatter.11.cloned.1.call-update) | async-done | bytes 1572880 | tf_op jit(solution)/shard_map/reduce_scatter | solution.py:250
  759.5 41.9 %reduce-scatter.7.cloned.1.call-done = bf16[2,128,1024]{2,1,0:T(8,128)(2,1)} async-done(((bf16[2,512,1024]{2,1,0:T(8,128)(2,1)}), bf16[2,128,1024]{2,1,0:T(8,128)(2,1)}) %reduce-scatter.7.cloned.1.call-update) | async-done | bytes 524304 | tf_op jit(solution)/shard_map/reduce_scatter | solution.py:151
  801.4 3.9 multiply_add_fusion
  805.3 40.1 %all-reduce.3 = (f32[1024]{0:T(1024)}, f32[1024]{0:T(1024)}, f32[1024]{0:T(1024)}, f32[1024]{0:T(1024)}, f32[1024]{0:T(1024)}) all-reduce(f32[1024]{0:T(1024)S(1)} %get-tuple-element.65, f32[1024]{0:T(1024)S(1)} %get-tuple-element.64, f32[1024]{0:T(1024)S(1)} %get-tuple-element.62, ...), channel_id=1, replica_groups=mesh['dp'=8,'mp'=4] {'dp','mp'}, use_global_device_ids=true, to_apply=%region_18.19 | all-reduce | flops 5120 | bytes 40960 | tf_op jit(solution)/shard_map/psum | solution.py:272
  (193 shorter events, 58.9 us)
Async XLA Ops:
  7.2 352.3 %copy-start = (bf16[1024,1024]{1,0:T(8,128)(2,1)S(1)}, bf16[1024,1024]{1,0:T(8,128)(2,1)}, u32[]{:S(2)}) copy-start(bf16[1024,1024]{1,0:T(8,128)(2,1)} %param.34) | copy-start | bytes 6291460
  7.2 51.1 %all-gather.9.cloned.1.call-start = ((), (), s32[]{:S(2)}) async-start(), calls=%async_computation.5 | async-start | bytes 2621440 | tf_op jit(solution)/shard_map/all_gather | solution.py:77
  7.9 96.6 %all-gather.7.cloned.1.call-start = ((), (), s32[]{:S(2)}) async-start(), calls=%async_computation.4 | async-start | bytes 2621440 | tf_op jit(solution)/shard_map/all_gather | solution.py:76
  8.7 142.1 %all-gather.11.cloned.1.call-start = ((), (), s32[]{:S(2)}) async-start(), calls=%async_computation.6 | async-start | bytes 2621440 | tf_op jit(solution)/shard_map/all_gather | solution.py:78
  9.4 254.4 %reduce-scatter.5.cloned.1.call-start = ((), (), s32[]{:S(2)}) async-start(), calls=%async_computation.7 | async-start | bytes 5242880 | tf_op jit(solution)/shard_map/reduce_scatter | solution.py:135
  150.8 5.0 copy-start.2
  150.8 5.0 copy-start.3
  150.8 5.0 copy-start.4
  155.7 5.5 copy-start.37
  155.7 5.5 copy-start.39
  161.2 5.2 copy-start.29
  161.2 6.0 copy-start.28
  167.2 5.1 copy-start.20
  169.2 3.1 copy-start.10
  175.6 4.5 copy-start.1
  180.1 5.3 copy-start.27
  188.1 77.5 %copy-start.36 = (f32[1024]{0:T(1024)S(1)}, f32[1024]{0:T(1024)}, u32[]{:S(2)}) copy-start(f32[1024]{0:T(1024)} %param.30) | copy-start | bytes 12292
  188.1 77.5 %copy-start.40 = (f32[1024]{0:T(1024)S(1)}, f32[1024]{0:T(1024)}, u32[]{:S(2)}) copy-start(f32[1024]{0:T(1024)} %param.31) | copy-start | bytes 12292
  188.2 125.1 %all-gather.13.cloned.1.call-start = ((), (), s32[]{:S(2)}) async-start(), calls=%async_computation.8 | async-start | bytes 2621440 | tf_op jit(solution)/shard_map/all_gather | solution.py:141
  266.7 92.8 %all-gather.15.cloned.1.call-start = ((), (), s32[]{:S(2)}) async-start(), calls=%async_computation.10 | async-start | bytes 2621440 | tf_op jit(solution)/shard_map/all_gather | solution.py:164
  267.3 92.2 %copy-start.46 = (f32[1024]{0:T(1024)S(1)}, f32[1024]{0:T(1024)}, u32[]{:S(2)}) copy-start(f32[1024]{0:T(1024)} %param.33) | copy-start | bytes 12292
  267.3 181.0 %reduce-scatter.9.cloned.1.call-start = ((), (), s32[]{:S(2)}) async-start(), calls=%async_computation.11 | async-start | bytes 5242880 | tf_op jit(solution)/shard_map/reduce_scatter | solution.py:179
  359.5 8.8 %copy-start.43 = (bf16[1024,1024]{1,0:T(8,128)(2,1)S(1)}, bf16[1024,1024]{1,0:T(8,128)(2,1)}, u32[]{:S(2)}) copy-start(bf16[1024,1024]{1,0:T(8,128)(2,1)} %param.32) | copy-start | bytes 6291460
  372.7 126.5 %all-gather.17.cloned.1.call-start = ((), (), s32[]{:S(2)}) async-start(), calls=%async_computation.12 | async-start | bytes 2621440 | tf_op jit(solution)/shard_map/all_gather | solution.py:190
  452.7 188.8 %all-reduce.7.cloned.1.call-start = ((), (), s32[]{:S(2)}) async-start(), calls=%async_computation.14 | async-start | bytes 12582912 | tf_op jit(solution)/shard_map/psum | solution.py:264
  453.1 6.1 copy-start.44
  453.1 6.1 copy-start.48
  501.6 7.1 copy-start.26
  501.7 16.6 %slice-start = ((s8[12582912]{0:T(1024)(128)(4,1)}), s8[4194304]{0:T(1024)(128)(4,1)S(1)}, s32[]{:S(2)}) async-start(s8[12582912]{0:T(1024)(128)(4,1)} %bitcast.155), calls=%async_computation.15 | async-start | bytes 8388608
  501.7 16.6 %slice-start.1 = ((s8[12582912]{0:T(1024)(128)(4,1)}), s8[4194304]{0:T(1024)(128)(4,1)S(1)}, s32[]{:S(2)}) async-start(s8[12582912]{0:T(1024)(128)(4,1)} %bitcast.155), calls=%async_computation.16 | async-start | bytes 8388608
  508.7 19.1 %copy-start.16 = (bf16[2,2,128,1536]{3,2,1,0:T(8,128)(2,1)}, bf16[2,2,128,1536]{3,2,1,0:T(8,128)(2,1)S(1)}, u32[]{:S(2)}) copy-start(bf16[2,2,128,1536]{3,2,1,0:T(8,128)(2,1)S(1)} %fusion.26) | copy-start | bytes 4718596
  508.7 9.5 %slice-start.2 = ((s8[12582912]{0:T(1024)(128)(4,1)}), s8[4194304]{0:T(1024)(128)(4,1)S(1)}, s32[]{:S(2)}) async-start(s8[12582912]{0:T(1024)(128)(4,1)} %bitcast.155), calls=%async_computation.17 | async-start | bytes 8388608
  518.2 6.4 copy-start.11
  524.7 3.2 slice-start.3
  526.8 4.5 copy-start.22
  527.9 5.0 copy-start.12
  537.1 217.5 %reduce-scatter.11.cloned.1.call-start = ((), (), s32[]{:S(2)}) async-start(), calls=%async_computation.13 | async-start | bytes 7864320 | tf_op jit(solution)/shard_map/reduce_scatter | solution.py:250
  537.3 3.5 copy-start.17
  537.4 3.5 copy-start.35
  540.9 6.4 copy-start.23
  540.9 6.4 copy-start.30
  567.6 233.7 %reduce-scatter.7.cloned.1.call-start = ((), (), s32[]{:S(2)}) async-start(), calls=%async_computation.9 | async-start | bytes 2621440 | tf_op jit(solution)/shard_map/reduce_scatter | solution.py:151
  612.9 5.3 copy-start.24
  612.9 5.3 copy-start.25
  641.4 6.4 copy-start.31
  641.4 7.5 copy-start.19
  647.9 3.7 copy-start.18
  756.9 44.4 %copy-start.41 = (f32[1024]{0:T(1024)S(1)}, f32[1024]{0:T(1024)}, u32[]{:S(2)}) copy-start(f32[1024]{0:T(1024)} %param.35) | copy-start | bytes 12292
  (17 other events, 34.3 us)
Sparse Core Ops, SparseCore 0:
  9.6 48.6 all-gather.8
  59.8 44.6 all-gather.6
  106.1 44.6 all-gather.10
  188.3 75.4 reduce-scatter.4
  266.8 46.4 all-gather.12
  314.8 44.6 all-gather.14
  372.8 75.4 reduce-scatter.8
  452.8 46.4 all-gather.16
  537.2 104.1 all-reduce.6
  643.7 110.8 reduce-scatter.10
  756.9 44.3 reduce-scatter.6
where the time goes:
time: 863 us; the launch traced here: 852 us
  waiting for transfers between devices  555 us (64%)
  matrix products  103 us (12%)
  other arithmetic  73.1 us (8%)
  blocking collectives  54.5 us (6%)
  local copies, waits for them, and re-layouts  49.8 us (6%)
  between operations  15.1 us (2%)
    reduce_scatter x1, waiting for transfers between devices, per_device(): lax.psum_scatter(partial_normed.astype(jnp.bfloat16), 'mp', scatter_dimen...  100 us
    reduce_scatter x1, waiting for transfers between devices, per_device(): lax.psum_scatter(partial_attn, 'mp', scatter_dimension=1, tiled=True)  75.6 us
    reduce_scatter x1, waiting for transfers between devices, per_device(): lax.psum_scatter(partial_second, 'mp', scatter_dimension=1, tiled=True)  75.6 us
    all_gather x1, waiting for transfers between devices, per_device(): lax.all_gather(tokens, 'mp', axis=1, tiled=True)  46.3 us
    all_gather x1, waiting for transfers between devices, per_device(): lax.all_gather(compressed, 'mp', axis=1, tiled=True)  46.3 us
    all_gather x1, waiting for transfers between devices, per_device(): second_all = lax.all_gather(feedforward_input, 'mp', axis=1, tiled=True)  46 us
    all_gather x1, waiting for transfers between devices, per_device(): lax.all_gather(memory, 'mp', axis=1, tiled=True)  45.5 us
    reduce_scatter x1, waiting for transfers between devices, per_device(): lax.psum_scatter(partial_ffn.astype(jnp.bfloat16), 'mp', scatter_dimensio...  41.9 us
  transfers between devices with their start and end apart: 11, of which 10 were waited for; matrix products, arithmetic and copies ran while one was open for 15% of the time, Pallas kernels for 0%

commit v1 on v0

--- a/solution.py
+++ b/solution.py
@@ -138,7 +138,12 @@
     feedforward_input = (
         standardized_feedforward * feedforward_norm_gain + feedforward_norm_bias
     ).astype(jnp.bfloat16)
-    second_all = lax.all_gather(feedforward_input, "mp", axis=1, tiled=True)
+    ring = [feedforward_input]
+    for hop in range(3):
+        ring.append(lax.ppermute(ring[-1], "mp", [(dev, (dev + 1) % 4) for dev in range(4)]))
+    second_all = jnp.roll(
+        jnp.concatenate(ring[::-1], axis=1), (lax.axis_index("mp") + 1) * ring[0].shape[1], axis=1
+    )
     upper_in = (
         jnp.einsum("gsd,df->gsf", second_all, up_weight, preferred_element_type=jnp.float32)
         + up_bias

time: 863 us -> 856 us (level)
  waiting for transfers between devices: 555 us -> 520 us
  starting transfers between devices: 1.31 us -> 22.4 us
    ppermute x0 -> x3, waiting for transfers between devices: none -> 51 us  [per_device(): lax.ppermute(ring[-1], 'mp', [(dev, (dev + 1) % 4) for dev in range(4)])]
    all_gather x1 -> x0, waiting for transfers between devices: 46 us -> none  [per_device(): second_all = lax.all_gather(feedforward_input, 'mp', axis=1, tiled=True)]
    all_gather x1, waiting for transfers between devices: 39.6 us -> 0.01 us  [per_device(): grad_all = lax.all_gather(cotangent, 'mp', axis=1, tiled=True)]
    ppermute x0 -> x3, starting transfers between devices: none -> 21.2 us  [per_device(): lax.ppermute(ring[-1], 'mp', [(dev, (dev + 1) % 4) for dev in range(4)])]
  transfers between devices with their start and end apart: 11 -> 13, of which waited for: 10 -> 11; matrix products, arithmetic and copies ran while one was open for 15% -> 15% of each run, Pallas kernels for 0% -> 0%
where the time goes in v1:
time: 856 us; the launch traced here: 845 us
  waiting for transfers between devices  520 us (61%)
  matrix products  101 us (12%)
  other arithmetic  73.7 us (9%)
  local copies, waits for them, and re-layouts  58.3 us (7%)
  blocking collectives  54.5 us (6%)
  starting transfers between devices  22.4 us (3%)
  between operations  15.5 us (2%)
    reduce_scatter x1, waiting for transfers between devices, per_device(): lax.psum_scatter(partial_normed.astype(jnp.bfloat16), 'mp', scatter_dimen...  101 us
    reduce_scatter x1, waiting for transfers between devices, per_device(): lax.psum_scatter(partial_attn, 'mp', scatter_dimension=1, tiled=True)  75.6 us
    reduce_scatter x1, waiting for transfers between devices, per_device(): lax.psum_scatter(partial_second, 'mp', scatter_dimension=1, tiled=True)  75.3 us
    ppermute x3, waiting for transfers between devices, per_device(): lax.ppermute(ring[-1], 'mp', [(dev, (dev + 1) % 4) for dev in range(4)])  51 us
    all_gather x1, waiting for transfers between devices, per_device(): lax.all_gather(tokens, 'mp', axis=1, tiled=True)  46.3 us
    all_gather x1, waiting for transfers between devices, per_device(): lax.all_gather(compressed, 'mp', axis=1, tiled=True)  46.3 us
    all_gather x1, waiting for transfers between devices, per_device(): lax.all_gather(memory, 'mp', axis=1, tiled=True)  45.5 us
    reduce_scatter x1, waiting for transfers between devices, per_device(): lax.psum_scatter(partial_ffn.astype(jnp.bfloat16), 'mp', scatter_dimensio...  41.7 us
  transfers between devices with their start and end apart: 13, of which 11 were waited for; matrix products, arithmetic and copies ran while one was open for 15% of the time, Pallas kernels for 0%

profile of v1, /device:TPU:0, one launch (start us, length us, event | category | flops | bytes accessed | tf_op | source)
XLA Modules:
  0.0 845.4 jit_solution(6419679631311055685)
XLA Ops:
  12.8 45.5 %all-gather.8.cloned.1.call-done = bf16[2,512,1024]{2,1,0:T(8,128)(2,1)} async-done(((bf16[2,128,1024]{2,1,0:T(8,128)(2,1)}), bf16[2,512,1024]{2,1,0:T(8,128)(2,1)}) %all-gather.8.cloned.1.call-update) | async-done | bytes 2097168 | tf_op jit(solution)/shard_map/all_gather | solution.py:77
  58.3 46.3 %all-gather.6.cloned.1.call-done = bf16[2,512,1024]{2,1,0:T(8,128)(2,1)} async-done(((bf16[2,128,1024]{2,1,0:T(8,128)(2,1)}), bf16[2,512,1024]{2,1,0:T(8,128)(2,1)}) %all-gather.6.cloned.1.call-update) | async-done | bytes 2097168 | tf_op jit(solution)/shard_map/all_gather | solution.py:76
  104.5 46.3 %all-gather.10.cloned.1.call-done = bf16[2,512,1024]{2,1,0:T(8,128)(2,1)} async-done(((bf16[2,128,1024]{2,1,0:T(8,128)(2,1)}), bf16[2,512,1024]{2,1,0:T(8,128)(2,1)}) %all-gather.10.cloned.1.call-update) | async-done | bytes 2097168 | tf_op jit(solution)/shard_map/all_gather | solution.py:78
  150.8 4.9 convert_reduce_fusion
  155.8 5.4 fusion.2
  161.2 5.2 fusion.5
  169.2 3.1 convolution_convert_fusion.1
  172.3 3.2 fusion.94
  180.1 4.4 fusion.61
  188.2 75.6 %reduce-scatter.5.cloned.1.call-done = f32[2,128,1024]{2,1,0:T(8,128)} async-done(((f32[2,512,1024]{2,1,0:T(8,128)}), f32[2,128,1024]{2,1,0:T(8,128)}) %reduce-scatter.5.cloned.1.call-update) | async-done | bytes 1048592 | tf_op jit(solution)/shard_map/reduce_scatter | solution.py:135
  268.2 17.2 %collective-permute-done = bf16[2,128,1024]{2,1,0:T(8,128)(2,1)} collective-permute-done((bf16[2,128,1024]{2,1,0:T(8,128)(2,1)}, bf16[2,128,1024]{2,1,0:T(8,128)(2,1)}, u32[]{:S(2)}, u32[]{:S(2)}) %collective-permute-start) | collective-permute-done | bytes 524320 | tf_op jit(solution)/shard_map/ppermute | solution.py:143
  285.4 4.6 collective-permute-start.1
  290.0 22.1 %collective-permute-done.1 = bf16[2,128,1024]{2,1,0:T(8,128)(2,1)} collective-permute-done((bf16[2,128,1024]{2,1,0:T(8,128)(2,1)}, bf16[2,128,1024]{2,1,0:T(8,128)(2,1)}, u32[]{:S(2)}, u32[]{:S(2)}) %collective-permute-start.1) | collective-permute-done | bytes 524320 | tf_op jit(solution)/shard_map/ppermute | solution.py:143
  312.1 15.1 %collective-permute-start.2 = (bf16[2,128,1024]{2,1,0:T(8,128)(2,1)}, bf16[2,128,1024]{2,1,0:T(8,128)(2,1)}, u32[]{:S(2)}, u32[]{:S(2)}) collective-permute-start(bf16[2,128,1024]{2,1,0:T(8,128)(2,1)} %collective-permute-done.1), channel_id=1, source_target_pairs={{0,1},{1,2},{2,3},{3,0},{4,5},{5,6},{6,7},{7,4},{8,9},{9,10},{10,1... | collective-permute-start | bytes 1572872 | tf_op jit(solution)/shard_map/ppermute | solution.py:143
  327.2 11.6 %collective-permute-done.2 = bf16[2,128,1024]{2,1,0:T(8,128)(2,1)} collective-permute-done((bf16[2,128,1024]{2,1,0:T(8,128)(2,1)}, bf16[2,128,1024]{2,1,0:T(8,128)(2,1)}, u32[]{:S(2)}, u32[]{:S(2)}) %collective-permute-start.2) | collective-permute-done | bytes 524320 | tf_op jit(solution)/shard_map/ppermute | solution.py:143
  348.0 4.4 fusion.34
  352.3 7.5 fusion.95
  361.2 4.4 fusion.32
  365.6 75.3 %reduce-scatter.9.cloned.1.call-done = f32[2,128,1024]{2,1,0:T(8,128)} async-done(((f32[2,512,1024]{2,1,0:T(8,128)}), f32[2,128,1024]{2,1,0:T(8,128)}) %reduce-scatter.9.cloned.1.call-update) | async-done | bytes 1048592 | tf_op jit(solution)/shard_map/reduce_scatter | solution.py:184
  445.8 6.1 bitcast_convert_fusion.1
  451.9 4.4 bitcast_convert_fusion
  456.3 35.6 %all-gather.14.cloned.1.call-done = bf16[2,512,1024]{2,1,0:T(8,128)(2,1)} async-done(((bf16[2,128,1024]{2,1,0:T(8,128)(2,1)}), bf16[2,512,1024]{2,1,0:T(8,128)(2,1)}) %all-gather.14.cloned.1.call-update) | async-done | bytes 2097168 | tf_op jit(solution)/shard_map/all_gather | solution.py:195
  494.3 7.0 fusion.26
  501.4 9.5 %multiply_reduce_fusion = (f32[2,2,512]{2,1,0:T(2,128)S(1)}, f32[2,2,512,1536]{3,2,1,0:T(8,128)}) fusion(f32[2,2,512,1536]{3,2,1,0:T(8,128)} %copy-done.1, f32[2,2,512]{2,1,0:T(2,128)S(1)} %log_add_fusion, bf16[2,512,2,128]{1,3,2,0:T(8,128)(2,1)S(1)} %bitcast.180, bf16[2,1536,2,128]{1,3,2,0:T(8,128)(2,1)S(1)} %bitcast.182), kind=kOutput, calls=%fused_computation.15 | convolution fusion | flops 814741504 | bytes 27279360 | tf_op jit(solution)/shard_map/gqhe,gkhe->ghqk/dot_general | solution.py:205
  510.9 6.4 multiply_convert_fusion
  530.0 3.5 fusion.67
  533.6 6.4 convolution_add_fusion
  540.0 5.0 fusion.21
  545.0 8.5 convert_element_type.161
  553.4 6.8 copy.66
  564.4 6.4 fusion.36
  571.2 3.9 concatenate.27
  575.1 8.2 while.4
  575.7 3.5 dynamic-slice_dynamic-update-slice_fusion.5
  579.8 3.5 dynamic-slice_dynamic-update-slice_fusion.5
  583.3 3.7 reshape.419
  587.0 6.3 fusion.51
  593.3 8.1 gather_fusion.1
  601.4 4.1 gather_fusion
  605.5 5.3 pad_maximum_fusion.1
  611.8 7.3 while.3
  612.4 3.0 dynamic-slice_dynamic-update-slice_fusion.4
  616.0 3.0 dynamic-slice_dynamic-update-slice_fusion.4
  619.1 14.4 %psum.93 = bf16[1024]{0:T(1024)(128)(2,1)S(1)} all-reduce(bf16[1024]{0:T(1024)(128)(2,1)S(1)} %get-tuple-element.121), channel_id=1, replica_groups=mesh['dp'=8,'mp'=4] {'dp'}, use_global_device_ids=true, to_apply=%region_31.32 | all-reduce | flops 1024 | bytes 4096 | tf_op jit(solution)/shard_map/psum | solution.py:274
  646.8 100.5 %reduce-scatter.11.cloned.1.call-done = bf16[2,3,128,1024]{3,2,0,1:T(8,128)(2,1)} async-done(((bf16[2,3,512,1024]{3,2,0,1:T(8,128)(2,1)}), bf16[2,3,128,1024]{3,2,0,1:T(8,128)(2,1)}) %reduce-scatter.11.cloned.1.call-update) | async-done | bytes 1572880 | tf_op jit(solution)/shard_map/reduce_scatter | solution.py:255
  752.3 41.7 %reduce-scatter.7.cloned.1.call-done = bf16[2,128,1024]{2,1,0:T(8,128)(2,1)} async-done(((bf16[2,512,1024]{2,1,0:T(8,128)(2,1)}), bf16[2,128,1024]{2,1,0:T(8,128)(2,1)}) %reduce-scatter.7.cloned.1.call-update) | async-done | bytes 524304 | tf_op jit(solution)/shard_map/reduce_scatter | solution.py:156
  794.0 3.9 multiply_add_fusion
  798.0 40.1 %all-reduce.3 = (f32[1024]{0:T(1024)}, f32[1024]{0:T(1024)}, f32[1024]{0:T(1024)}, f32[1024]{0:T(1024)}, f32[1024]{0:T(1024)}) all-reduce(f32[1024]{0:T(1024)S(1)} %get-tuple-element.65, f32[1024]{0:T(1024)S(1)} %get-tuple-element.64, f32[1024]{0:T(1024)S(1)} %get-tuple-element.62, ...), channel_id=1, replica_groups=mesh['dp'=8,'mp'=4] {'dp','mp'}, use_global_device_ids=true, to_apply=%region_18.19 | all-reduce | flops 5120 | bytes 40960 | tf_op jit(solution)/shard_map/psum | solution.py:277
  (208 shorter events, 77.1 us)
Async XLA Ops:
  7.2 345.2 %copy-start = (bf16[1024,1024]{1,0:T(8,128)(2,1)S(1)}, bf16[1024,1024]{1,0:T(8,128)(2,1)}, u32[]{:S(2)}) copy-start(bf16[1024,1024]{1,0:T(8,128)(2,1)} %param.34) | copy-start | bytes 6291460
  7.2 51.1 %all-gather.8.cloned.1.call-start = ((), (), s32[]{:S(2)}) async-start(), calls=%async_computation.5 | async-start | bytes 2621440 | tf_op jit(solution)/shard_map/all_gather | solution.py:77
  7.9 96.6 %all-gather.6.cloned.1.call-start = ((), (), s32[]{:S(2)}) async-start(), calls=%async_computation.4 | async-start | bytes 2621440 | tf_op jit(solution)/shard_map/all_gather | solution.py:76
  8.7 142.1 %all-gather.10.cloned.1.call-start = ((), (), s32[]{:S(2)}) async-start(), calls=%async_computation.6 | async-start | bytes 2621440 | tf_op jit(solution)/shard_map/all_gather | solution.py:78
  9.4 254.3 %reduce-scatter.5.cloned.1.call-start = ((), (), s32[]{:S(2)}) async-start(), calls=%async_computation.7 | async-start | bytes 5242880 | tf_op jit(solution)/shard_map/reduce_scatter | solution.py:135
  150.8 5.0 copy-start.2
  150.8 5.0 copy-start.3
  150.8 5.0 copy-start.4
  155.7 5.5 copy-start.39
  155.7 5.5 copy-start.41
  161.2 5.2 copy-start.29
  161.2 6.0 copy-start.28
  167.2 5.1 copy-start.20
  175.6 4.5 copy-start.1
  180.1 5.2 copy-start.27
  188.1 77.5 %copy-start.36 = (f32[1024]{0:T(1024)S(1)}, f32[1024]{0:T(1024)}, u32[]{:S(2)}) copy-start(f32[1024]{0:T(1024)} %param.30) | copy-start | bytes 12292
  188.1 77.5 %copy-start.38 = (f32[1024]{0:T(1024)S(1)}, f32[1024]{0:T(1024)}, u32[]{:S(2)}) copy-start(f32[1024]{0:T(1024)} %param.31) | copy-start | bytes 12292
  188.1 164.2 %all-gather.12.cloned.1.call-start = ((), (), s32[]{:S(2)}) async-start(), calls=%async_computation.9 | async-start | bytes 2621440 | tf_op jit(solution)/shard_map/all_gather | solution.py:169
  266.6 18.8 %collective-permute-start = (bf16[2,128,1024]{2,1,0:T(8,128)(2,1)}, bf16[2,128,1024]{2,1,0:T(8,128)(2,1)}, u32[]{:S(2)}, u32[]{:S(2)}) collective-permute-start(bf16[2,128,1024]{2,1,0:T(8,128)(2,1)} %add_convert_fusion.1), channel_id=1, source_target_pairs={{0,1},{1,2},{2,3},{3,0},{4,5},{5,6},{6,7},{7,4},{8,9},{9,10},{10,1... | collective-permute-start | bytes 1572872 | tf_op jit(solution)/shard_map/ppermute | solution.py:143
  268.1 172.8 %reduce-scatter.9.cloned.1.call-start = ((), (), s32[]{:S(2)}) async-start(), calls=%async_computation.10 | async-start | bytes 5242880 | tf_op jit(solution)/shard_map/reduce_scatter | solution.py:184
  285.4 26.7 %collective-permute-start.1 = (bf16[2,128,1024]{2,1,0:T(8,128)(2,1)}, bf16[2,128,1024]{2,1,0:T(8,128)(2,1)}, u32[]{:S(2)}, u32[]{:S(2)}) collective-permute-start(bf16[2,128,1024]{2,1,0:T(8,128)(2,1)} %collective-permute-done), channel_id=1, source_target_pairs={{0,1},{1,2},{2,3},{3,0},{4,5},{5,6},{6,7},{7,4},{8,9},{9,10},{10,1... | collective-permute-start | bytes 1572872 | tf_op jit(solution)/shard_map/ppermute | solution.py:143
  312.1 26.8 %collective-permute-start.2 = (bf16[2,128,1024]{2,1,0:T(8,128)(2,1)}, bf16[2,128,1024]{2,1,0:T(8,128)(2,1)}, u32[]{:S(2)}, u32[]{:S(2)}) collective-permute-start(bf16[2,128,1024]{2,1,0:T(8,128)(2,1)} %collective-permute-done.1), channel_id=1, source_target_pairs={{0,1},{1,2},{2,3},{3,0},{4,5},{5,6},{6,7},{7,4},{8,9},{9,10},{10,1... | collective-permute-start | bytes 1572872 | tf_op jit(solution)/shard_map/ppermute | solution.py:143
  340.0 8.0 copy-start.44
  348.0 4.4 copy-start.48
  352.3 8.8 %copy-start.45 = (bf16[1024,1024]{1,0:T(8,128)(2,1)S(1)}, bf16[1024,1024]{1,0:T(8,128)(2,1)}, u32[]{:S(2)}) copy-start(bf16[1024,1024]{1,0:T(8,128)(2,1)} %param.32) | copy-start | bytes 6291460
  365.6 126.3 %all-gather.14.cloned.1.call-start = ((), (), s32[]{:S(2)}) async-start(), calls=%async_computation.11 | async-start | bytes 2621440 | tf_op jit(solution)/shard_map/all_gather | solution.py:195
  445.3 188.8 %all-reduce.7.cloned.1.call-start = ((), (), s32[]{:S(2)}) async-start(), calls=%async_computation.13 | async-start | bytes 12582912 | tf_op jit(solution)/shard_map/psum | solution.py:269
  445.8 6.1 copy-start.46
  445.8 6.1 copy-start.50
  494.3 7.1 copy-start.26
  494.3 16.6 %slice-start = ((s8[12582912]{0:T(1024)(128)(4,1)}), s8[4194304]{0:T(1024)(128)(4,1)S(1)}, s32[]{:S(2)}) async-start(s8[12582912]{0:T(1024)(128)(4,1)} %bitcast.153), calls=%async_computation.14 | async-start | bytes 8388608
  494.3 16.6 %slice-start.1 = ((s8[12582912]{0:T(1024)(128)(4,1)}), s8[4194304]{0:T(1024)(128)(4,1)S(1)}, s32[]{:S(2)}) async-start(s8[12582912]{0:T(1024)(128)(4,1)} %bitcast.153), calls=%async_computation.15 | async-start | bytes 8388608
  501.4 19.2 %copy-start.16 = (bf16[2,2,128,1536]{3,2,1,0:T(8,128)(2,1)}, bf16[2,2,128,1536]{3,2,1,0:T(8,128)(2,1)S(1)}, u32[]{:S(2)}) copy-start(bf16[2,2,128,1536]{3,2,1,0:T(8,128)(2,1)S(1)} %fusion.26) | copy-start | bytes 4718596
  501.4 9.5 %slice-start.2 = ((s8[12582912]{0:T(1024)(128)(4,1)}), s8[4194304]{0:T(1024)(128)(4,1)S(1)}, s32[]{:S(2)}) async-start(s8[12582912]{0:T(1024)(128)(4,1)} %bitcast.153), calls=%async_computation.16 | async-start | bytes 8388608
  510.9 6.4 copy-start.11
  519.5 4.5 copy-start.22
  520.5 5.0 copy-start.12
  529.7 217.6 %reduce-scatter.11.cloned.1.call-start = ((), (), s32[]{:S(2)}) async-start(), calls=%async_computation.12 | async-start | bytes 7864320 | tf_op jit(solution)/shard_map/reduce_scatter | solution.py:255
  530.0 3.5 copy-start.17
  533.6 6.4 copy-start.23
  533.6 6.4 copy-start.30
  560.3 233.8 %reduce-scatter.7.cloned.1.call-start = ((), (), s32[]{:S(2)}) async-start(), calls=%async_computation.8 | async-start | bytes 2621440 | tf_op jit(solution)/shard_map/reduce_scatter | solution.py:156
  605.5 5.3 copy-start.24
  605.5 5.4 copy-start.25
  634.1 6.4 copy-start.31
  634.1 7.5 copy-start.19
  640.5 3.8 copy-start.18
  749.7 44.3 %copy-start.42 = (f32[1024]{0:T(1024)S(1)}, f32[1024]{0:T(1024)}, u32[]{:S(2)}) copy-start(f32[1024]{0:T(1024)} %param.35) | copy-start | bytes 12292
  (21 other events, 46.2 us)
Sparse Core Ops, SparseCore 0:
  9.6 48.6 all-gather.7
  59.8 44.6 all-gather.5
  106.1 44.6 all-gather.9
  188.2 75.4 reduce-scatter.4
  268.2 61.7 all-gather.11
  365.7 75.2 reduce-scatter.8
  445.4 46.4 all-gather.13
  529.9 104.1 all-reduce.6
  636.5 110.8 reduce-scatter.10
  749.6 44.3 reduce-scatter.6
